TPU v7x, 32 devices: a whole 2x2x4 slice. The times are simulated.
32 devices in a mesh: dp: 4 (over z), expert: 8 (over y, x, core).
Axes of the slice: x: 2, y: 2, z: 4, core: 2. Of those that a mesh axis runs over, the one named last changes fastest.
Arguments:
- queries: bfloat16 [8192, 1536], P(('dp', 'expert')), may hold values from -8 to 8
- rotated_key_heads: bfloat16 [8192, 512], P(('dp', 'expert')), may hold values from -8 to 8
- token_value_heads: bfloat16 [8192, 512], P(('dp', 'expert')), may hold values from -4 to 4
- residual: bfloat16 [8192, 1536], P(('dp', 'expert')), may hold values from -20 to 20
- lengths: int32 [32, 4], P(('dp', 'expert')), may hold values from 1 to 128, 256 in all within a row
- request_adapter_index: int32 [128], P(('dp', 'expert')), may hold values from 0 to 63
- attention_output_weight: bfloat16 [1536, 1536], P('dp'), may hold values from -0.15625 to 0.15625
- adapter_down_factor: bfloat16 [64, 1536, 16], P('expert'), may hold values from -0.15625 to 0.15625
- adapter_up_factor: bfloat16 [64, 16, 1536], P('expert'), may hold values from -1.5 to 1.5
- expert_norm_scale: float32 [1536], replicated, may hold values from 0.5 to 1.5
- router_logit_scores: float32 [8192, 8], P(('dp', 'expert')), may hold values from -4 to 404
- routes: int32 [8192, 8], P(('dp', 'expert')), may hold values from 0 to 15, all different within a row; in each aligned block of 256 rows (0 to 255, 256 to 511, ...) at most 160 rows name the same one
- expert_gate_weight: bfloat16 [16, 1536, 512], P('expert'), may hold values from -0.15625 to 0.15625
- expert_up_weight: bfloat16 [16, 1536, 512], P('expert'), may hold values from -0.15625 to 0.15625
- expert_down_weight: bfloat16 [16, 512, 1536], P('expert'), may hold values from -0.25 to 0.25
Outputs:
- block_out: bfloat16 [8192, 1536], P(('dp', 'expert'))
Inputs may be any that keep to these rules, and one draw needn't show every extreme that they name: `routes`: in the rows of one device no expert is named by more than 160 rows, a bound that some block reaches.
All inputs are finite; a program needn't handle non-finite values.
Results may differ from a plain program's by a relative error of at most 0.0044.
Values may be sent and summed in bfloat16 or wider, within the bound.
No kernel may reach another device: no remote copies, remote signals or barrier semaphores. Data moves between devices by JAX's collectives and lax.ppermute only.
A program may use at most 128 MiB of HBM per device.

v0:
```python
import jax
import jax.numpy as jnp
from jax import lax
from jax.sharding import PartitionSpec as P

HEADS = 24
KV_HEADS = 8
HEAD = 64
TOPK = 8


def segment_of(lengths_row, tokens):
    request_ends = jnp.cumsum(lengths_row)
    positions = jnp.arange(tokens, dtype=jnp.int32)
    return jnp.sum((positions[:, None] >= request_ends[None, :]).astype(jnp.int32), axis=1)


def attend(queries, rotated_key_heads, token_value_heads, segment):
    tokens = queries.shape[0]
    groups = HEADS // KV_HEADS
    grouped = queries.reshape(tokens, KV_HEADS, groups, HEAD)
    key_heads = rotated_key_heads.reshape(tokens, KV_HEADS, HEAD)
    value_heads = token_value_heads.reshape(tokens, KV_HEADS, HEAD)
    scores = jnp.einsum(
        "tkgh,skh->kgts", grouped, key_heads, preferred_element_type=jnp.float32
    ) * HEAD ** (-0.5)
    positions = jnp.arange(tokens, dtype=jnp.int32)
    allowed = (segment[:, None] == segment[None, :]) & (positions[:, None] >= positions[None, :])
    scores = jnp.where(allowed, scores, -1e30)
    row_peak = jnp.max(scores, axis=-1, keepdims=True)
    raised = jnp.exp(scores - row_peak)
    weights = (raised / jnp.sum(raised, axis=-1, keepdims=True)).astype(jnp.bfloat16)
    head_mix = jnp.einsum(
        "kgts,skh->tkgh", weights, value_heads, preferred_element_type=jnp.float32
    )
    return head_mix.reshape(tokens, HEADS * HEAD).astype(jnp.bfloat16)


def run_experts(arrived, expert_gate_weight, expert_up_weight, expert_down_weight):
    gate_part = jnp.einsum(
        "secd,edf->secf", arrived, expert_gate_weight, preferred_element_type=jnp.float32
    )
    up_part = jnp.einsum(
        "secd,edf->secf", arrived, expert_up_weight, preferred_element_type=jnp.float32
    )
    active = (jax.nn.silu(gate_part) * up_part).astype(jnp.bfloat16)
    return jnp.einsum(
        "secf,efd->secd", active, expert_down_weight, preferred_element_type=jnp.float32
    ).astype(jnp.bfloat16)


def per_device(
    queries,
    rotated_key_heads,
    token_value_heads,
    residual,
    lengths,
    request_adapter_index,
    attention_output_weight,
    adapter_down_factor,
    adapter_up_factor,
    expert_norm_scale,
    router_logit_scores,
    routes,
    expert_gate_weight,
    expert_up_weight,
    expert_down_weight,
):
    tokens = queries.shape[0]
    width = attention_output_weight.shape[1]
    requests_here = request_adapter_index.shape[0]
    segment = segment_of(lengths[0], tokens)
    context = attend(queries, rotated_key_heads, token_value_heads, segment)
    projected = jnp.dot(
        context,
        lax.all_gather(attention_output_weight, "dp", axis=0, tiled=True),
        preferred_element_type=jnp.float32,
    )
    member_int = (segment[:, None] == jnp.arange(requests_here, dtype=jnp.int32)[None, :]).astype(
        jnp.int32
    )
    pool_down, pool_up = (
        lax.all_gather(adapter_down_factor, "expert", axis=0, tiled=True),
        lax.all_gather(adapter_up_factor, "expert", axis=0, tiled=True),
    )
    chosen_down = jnp.take(pool_down, request_adapter_index, axis=0)
    chosen_up = jnp.take(pool_up, request_adapter_index, axis=0)
    rank_size = chosen_down.shape[2]
    every_low = jnp.einsum("td,rdk->trk", context, chosen_down, preferred_element_type=jnp.float32)
    picked_low = (every_low * member_int.astype(jnp.float32)[:, :, None]).astype(jnp.bfloat16)
    picked_low = picked_low.reshape(tokens, requests_here * rank_size)
    adapter_term = jnp.dot(
        picked_low,
        chosen_up.reshape(requests_here * rank_size, width),
        preferred_element_type=jnp.float32,
    )
    hidden = residual.astype(jnp.float32) + projected + adapter_term
    mean_square = jnp.mean(hidden * hidden, axis=-1, keepdims=True)
    normed = (hidden * lax.rsqrt(mean_square + 1e-06) * expert_norm_scale).astype(jnp.bfloat16)
    logit_peak = jnp.max(router_logit_scores, axis=-1, keepdims=True)
    raised = jnp.exp(router_logit_scores - logit_peak)
    gate_weights = raised / jnp.sum(raised, axis=-1, keepdims=True)
    local_experts = expert_gate_weight.shape[0]
    expert_devices = lax.axis_size("expert")
    experts_all = local_experts * expert_devices
    capacity = min(tokens, max(2, tokens * TOPK * 5 // (4 * experts_all)))
    flat_routes = routes.reshape(-1)
    route_hits = (flat_routes[:, None] == jnp.arange(experts_all, dtype=jnp.int32)[None, :]).astype(
        jnp.int32
    )
    slot_rank = jnp.sum((jnp.cumsum(route_hits, axis=0) - route_hits) * route_hits, axis=1)
    slot_index = flat_routes * capacity + slot_rank
    anchor = jnp.arange(tokens * TOPK, dtype=jnp.int32) // TOPK
    sources = jnp.zeros((experts_all * capacity,), jnp.int32).at[slot_index].set(anchor)
    filled = jnp.zeros((experts_all * capacity,), jnp.int32).at[slot_index].set(1)
    outgoing = jnp.where(
        filled[:, None] > 0, jnp.take(normed, sources, axis=0), jnp.zeros((), normed.dtype)
    )
    outgoing = outgoing.reshape(expert_devices, local_experts, capacity, width)
    arrived = lax.all_to_all(outgoing, "expert", split_axis=0, concat_axis=0, tiled=True)
    came_back = lax.all_to_all(
        run_experts(arrived, expert_gate_weight, expert_up_weight, expert_down_weight),
        "expert",
        split_axis=0,
        concat_axis=0,
        tiled=True,
    )
    picked = jnp.take(came_back.reshape(experts_all * capacity, width), slot_index, axis=0).reshape(
        tokens, TOPK, width
    )
    mixture = jnp.sum(gate_weights[:, :, None] * picked, axis=1)
    return (hidden + mixture).astype(jnp.bfloat16)


def solution(mesh):
    return jax.shard_map(
        per_device,
        mesh=mesh,
        in_specs=(
            P(("dp", "expert"), None),
            P(("dp", "expert"), None),
            P(("dp", "expert"), None),
            P(("dp", "expert"), None),
            P(("dp", "expert"), None),
            P(("dp", "expert")),
            P("dp", None),
            P("expert", None, None),
            P("expert", None, None),
            P(),
            P(("dp", "expert"), None),
            P(("dp", "expert"), None),
            P("expert", None, None),
            P("expert", None, None),
            P("expert", None, None),
        ),
        out_specs=P(("dp", "expert"), None),
        check_vma=False,
    )
```

profile of v0, /device:TPU:0, one launch (start us, length us, event | category | flops | bytes accessed | tf_op | source)
XLA Modules:
  0.0 456.1 jit_solution(2554271354359313261)
XLA Ops:
  6.5 0.0 copy-start
  6.5 0.7 all-gather.6.cloned.1.call-update
  7.3 0.0 all-gather.8.cloned.1.call-start
  7.3 0.7 all-gather.8.cloned.1.call-update
  8.0 0.0 all-gather.4.cloned.1.call-start
  8.1 0.7 all-gather.4.cloned.1.call-update
  8.7 0.8 copy.64
  9.6 0.1 eq.62
  9.7 0.1 reshape.168
  9.8 2.3 copy.59
  12.1 1.8 copy.58
  13.9 1.8 copy.60
  15.7 0.8 reduce-window.18
  16.5 4.5 reduce-window.19
  21.1 0.4 slice_reduce_fusion
  21.5 0.2 reduce-window.20
  21.7 0.1 copy.68
  21.8 0.1 mul.82
  22.0 0.1 broadcast_add_fusion
  22.1 0.1 fusion.34
  22.2 8.1 %scatter_custom_fusion.1 = s32[2560]{0:T(1024)S(1)} fusion(s32[2048]{0:T(1024)S(1)} %bitcast.120, s32[2048]{0:T(1024)S(1)} %add_select_fusion, s32[]{:T(128)} %constant.64.clone.1), kind=kCustom, calls=%fused_computation.74 | custom fusion | bytes 10244 | tf_op jit(solution)/shard_map/scatter | solution.py:114
  30.2 0.7 broadcast_in_dim.102
  30.9 8.1 %scatter_custom_fusion = s32[2560]{0:T(1024)S(1)} fusion(s32[2048]{0:T(1024)S(1)} %bitcast.121, s32[2048]{0:T(1024)S(1)} %broadcast.140, s32[]{:T(128)} %constant.64.clone.1), kind=kCustom, calls=%fused_computation.77 | custom fusion | bytes 10244 | tf_op jit(solution)/shard_map/scatter | solution.py:115
  39.0 0.7 broadcast_in_dim.100
  39.7 0.6 pad_clamp_fusion
  40.3 0.1 convert_reduce_fusion
  40.4 0.5 compare_and_fusion.2
  40.9 0.6 convert_convert_fusion
  41.5 0.1 fusion.29
  41.6 0.0 copy-start.5
  41.6 6.0 %fusion.51 = (f32[8,3,256]{2,1,0:T(4,128)S(1)}, f32[8,3,256,256]{2,3,1,0:T(8,128)}) fusion(pred[256,256]{0,1:T(8,128)(4,1)S(1)} %fusion.29, bf16[256,8,64,1]{0,2,3,1:T(8,128)(2,1)} %bitcast.117, bf16[256,8,3,64]{0,3,2,1:T(8,128)(2,1)} %bitcast.114), kind=kOutput, calls=%fused_computation.93 | convolution fusion | flops 207618304 | bytes 7430144 | tf_op jit(solution)/shard_map/sub | solution.py:31
  47.6 4.3 fusion.26
  52.0 0.0 copy-done.14
  52.0 2.6 gather_fusion
  54.6 24.0 %all-gather.8.cloned.1.call-done = bf16[64,16,1536]{2,1,0:T(8,128)(2,1)} async-done(((bf16[8,16,1536]{2,1,0:T(8,128)(2,1)}), bf16[64,16,1536]{2,1,0:T(8,128)(2,1)}) %all-gather.8.cloned.1.call-update) | async-done | bytes 3145744 | tf_op jit(solution)/shard_map/all_gather | solution.py:84
  78.6 2.6 gather_fusion.1
  81.2 0.7 broadcast_select_fusion
  81.8 1.4 fusion.52
  83.2 2.3 convolution_bitcast_fusion
  85.5 84.1 %all-gather.4.cloned.1.call-done = bf16[1536,1536]{1,0:T(8,128)(2,1)} async-done(((bf16[384,1536]{1,0:T(8,128)(2,1)}), bf16[1536,1536]{1,0:T(8,128)(2,1)}) %all-gather.4.cloned.1.call-update) | async-done | bytes 4718608 | tf_op jit(solution)/shard_map/all_gather | solution.py:76
  169.6 4.8 %multiply_reduce_fusion.1 = (f32[256]{0:T(256)S(1)}, f32[256,1536]{1,0:T(8,128)S(1)}) fusion(f32[256,1536]{1,0:T(8,128)} %convolution_bitcast_fusion, bf16[256,1536]{0,1:T(8,128)(2,1)} %bitcast.112, bf16[1536,1536]{1,0:T(8,128)(2,1)} %all-gather.4.cloned.1.call-done, bf16[256,1536]{1,0:T(8,128)(2,1)} %param.18), kind=kOutput, calls=%fused_computation.38 | convolution fusion | flops 1209925376 | bytes 9438208 | tf_op jit(solution)/shard_map/dot_general | solution.py:74
  174.4 0.0 copy-start.2
  174.4 1.2 copy-done.2
  175.6 1.1 multiply_convert_fusion
  176.6 17.6 %gather_fusion.2 = bf16[2560,1536]{1,0:T(8,128)(2,1)} fusion(bf16[256,1536]{1,0:T(8,128)(2,1)} %multiply_convert_fusion, s32[3072]{0:T(1024)S(1)} %copy-done.8), kind=kCustom, calls=%fused_computation.2 | custom fusion | bytes 15738880 | tf_op jit(solution)/shard_map/jit(_take)/gather | solution.py:117
  194.3 0.0 copy-done.10
  194.3 4.5 select_select_fusion
  198.7 0.0 copy-start.15
  198.7 92.1 %all_to_all.10 = bf16[8,2,160,1536]{3,2,1,0:T(8,128)(2,1)S(1)} all-to-all(bf16[8,2,160,1536]{3,2,1,0:T(8,128)(2,1)S(1)} %select_select_fusion), channel_id=1, replica_groups=mesh['dp'=4,'expert'=8] {'expert'}, dimensions={0} | all-to-all | bytes 15728640 | tf_op jit(solution)/shard_map/all_to_all | solution.py:120
  290.9 3.2 copy-done.4
  294.0 0.0 copy-done.15
  294.1 5.9 %fusion.1 = f32[2,8,160,512]{3,2,1,0:T(8,128)} fusion(bf16[8,2,160,1536]{3,2,1,0:T(8,128)(2,1)S(1)} %all_to_all.10, bf16[2,1536,512]{2,1,0:T(8,128)(2,1)S(1)} %copy-done.15), kind=kOutput, calls=%fused_computation.10 | convolution fusion | flops 4026531840 | bytes 16252928 | tf_op jit(solution)/shard_map/secd,edf->secf/dot_general | solution.py:43
  300.0 14.2 %convert_bitcast_fusion = bf16[8,2,160,1536]{3,2,0,1:T(8,128)(2,1)} fusion(bf16[2,512,1536]{2,1,0:T(8,128)(2,1)S(1)} %copy-done, f32[2,8,160,512]{3,2,1,0:T(8,128)} %fusion.1, bf16[2,1536,512]{2,1,0:T(8,128)(2,1)} %param.27, bf16[8,2,160,1536]{3,2,1,0:T(8,128)(2,1)} %copy-done.4), kind=kOutput, calls=%fused_computation.8 | convolution fusion | flops 8064860160 | bytes 27262976 | tf_op jit(solution)/shard_map/secf,efd->secd/dot_general | solution.py:47
  314.2 7.1 %copy.71 = bf16[8,2,160,1536]{3,2,1,0:T(8,128)(2,1)} copy(bf16[8,2,160,1536]{3,2,0,1:T(8,128)(2,1)} %convert_bitcast_fusion) | data formatting | bytes 15728640 | tf_op jit(solution)/shard_map/convert_element_type | solution.py:49
  321.3 5.0 %all-to-all-start.1 = ((bf16[8,2,160,1536]{3,2,1,0:T(8,128)(2,1)}), bf16[8,2,160,1536]{3,2,1,0:T(8,128)(2,1)}, u32[]{:S(2)}, u32[]{:S(2)}) async-start(bf16[8,2,160,1536]{3,2,1,0:T(8,128)(2,1)} %copy.71), calls=%async_computation.1 | async-start | bytes 15728640 | tf_op jit(solution)/shard_map/all_to_all | solution.py:121
  326.3 0.1 reduce_sum.62
  326.4 0.1 copy.66
  326.5 0.2 copy.67
  326.7 0.0 copy-done.7
  326.8 0.1 copy.63
  326.9 87.9 %all-to-all-done.1 = bf16[8,2,160,1536]{3,2,1,0:T(8,128)(2,1)} async-done(((bf16[8,2,160,1536]{3,2,1,0:T(8,128)(2,1)}), bf16[8,2,160,1536]{3,2,1,0:T(8,128)(2,1)}, u32[]{:S(2)}, u32[]{:S(2)}) %all-to-all-start.1) | async-done | bytes 7864352 | tf_op jit(solution)/shard_map/all_to_all | solution.py:121
  414.8 17.7 %gather_fusion.3 = bf16[2048,1536]{1,0:T(8,128)(2,1)} fusion(bf16[2560,1536]{1,0:T(8,128)(2,1)} %bitcast.30, s32[2048]{0:T(1024)S(1)} %broadcast_clamp_fusion), kind=kCustom, calls=%fused_computation.3 | custom fusion | bytes 12591104 | tf_op jit(solution)/shard_map/jit(_take)/gather | solution.py:128
  432.5 16.0 %multiply_reduce_fusion = f32[256,1536]{1,0:T(8,128)S(1)} fusion(bf16[2048,1536]{1,0:T(8,128)(2,1)} %gather_fusion.3, f32[256,8]{1,0:T(8,128)S(1)} %copy.63, pred[256,8]{1,0:T(8,128)(4,1)S(1)} %copy.67), kind=kLoop, calls=%fused_computation.7 | loop fusion | flops 12189696 | bytes 7874560 | tf_op jit(solution)/shard_map/reduce_sum | solution.py:131
  448.5 1.1 add_convert_fusion
  (42 shorter events, 0.2 us)
Async XLA Ops:
  6.5 293.4 %copy-start = (bf16[2,512,1536]{2,1,0:T(8,128)(2,1)S(1)}, bf16[2,512,1536]{2,1,0:T(8,128)(2,1)}, u32[]{:S(2)}) copy-start(bf16[2,512,1536]{2,1,0:T(8,128)(2,1)} %param.29) | copy-start | bytes 9437188
  6.5 15.1 %copy-start.6 = (s32[256,8]{0,1:T(8,128)S(1)}, s32[256,8]{0,1:T(8,128)}, u32[]{:S(2)}) copy-start(s32[256,8]{0,1:T(8,128)} %param.26) | copy-start | bytes 24580
  6.5 33.1 %copy-start.16 = (s32[4]{0:T(128)S(1)}, s32[4]{0:T(128)}, u32[]{:S(2)}) copy-start(s32[4]{0:T(128)} %param.20) | copy-start | bytes 52
  6.5 45.4 %all-gather.6.cloned.1.call-start = ((), (), s32[]{:S(2)}) async-start(), calls=%async_computation.3 | async-start | bytes 3538944 | tf_op jit(solution)/shard_map/all_gather | solution.py:83
  7.3 71.3 %all-gather.8.cloned.1.call-start = ((), (), s32[]{:S(2)}) async-start(), calls=%async_computation.4 | async-start | bytes 3538944 | tf_op jit(solution)/shard_map/all_gather | solution.py:84
  8.0 161.6 %all-gather.4.cloned.1.call-start = ((), (), s32[]{:S(2)}) async-start(), calls=%async_computation.2 | async-start | bytes 5898240 | tf_op jit(solution)/shard_map/all_gather | solution.py:76
  22.2 18.8 %copy-start.11 = (s32[2048,1]{0,1:T(1,128)}, s32[2048,1]{0,1:T(1,128)S(1)}, u32[]{:S(2)}) copy-start(s32[2048,1]{0,1:T(1,128)S(1)} %compare_select_fusion) | copy-start | bytes 24580
  39.7 12.3 %copy-start.14 = (s32[1024]{0:T(1024)}, s32[1024]{0:T(1024)S(1)}, u32[]{:S(2)}) copy-start(s32[1024]{0:T(1024)S(1)} %pad_clamp_fusion.1) | copy-start | bytes 12292
  41.6 6.0 %copy-start.5 = (bf16[256,512]{0,1:T(8,128)(2,1)S(1)}, bf16[256,512]{0,1:T(8,128)(2,1)}, u32[]{:S(2)}) copy-start(bf16[256,512]{0,1:T(8,128)(2,1)} %copy.60) | copy-start | bytes 786436
  85.5 90.1 %copy-start.13 = (f32[1536]{0:T(1024)S(1)}, f32[1536]{0:T(1024)}, u32[]{:S(2)}) copy-start(f32[1536]{0:T(1024)} %param.24) | copy-start | bytes 18436
  85.5 91.1 %copy-start.8 = (s32[3072]{0:T(1024)S(1)}, s32[3072]{0:T(1024)}, u32[]{:S(2)}) copy-start(s32[3072]{0:T(1024)} %pad_clamp_fusion) | copy-start | bytes 36868
  174.4 1.2 copy-start.2
  176.6 17.6 %copy-start.9 = (pred[8,2,160]{2,1,0:T(4,128)(4,1)S(1)}, pred[8,2,160]{2,1,0:T(4,128)(4,1)}, u32[]{:S(2)}) copy-start(pred[8,2,160]{2,1,0:T(4,128)(4,1)} %broadcast_in_dim.102) | copy-start | bytes 7684
  176.6 17.6 %copy-start.10 = (pred[8,2,160]{2,1,0:T(4,128)(4,1)S(1)}, pred[8,2,160]{2,1,0:T(4,128)(4,1)}, u32[]{:S(2)}) copy-start(pred[8,2,160]{2,1,0:T(4,128)(4,1)} %broadcast_in_dim.100) | copy-start | bytes 7684
  198.7 95.3 %copy-start.15 = (bf16[2,1536,512]{2,1,0:T(8,128)(2,1)S(1)}, bf16[2,1536,512]{2,1,0:T(8,128)(2,1)}, u32[]{:S(2)}) copy-start(bf16[2,1536,512]{2,1,0:T(8,128)(2,1)} %param.28) | copy-start | bytes 9437188
  290.9 3.2 copy-start.4
  321.3 5.4 %copy-start.7 = (f32[256,8]{0,1:T(8,128)S(1)}, f32[256,8]{0,1:T(8,128)}, u32[]{:S(2)}) copy-start(f32[256,8]{0,1:T(8,128)} %param.25) | copy-start | bytes 24580
  321.3 5.6 %copy-start.12 = (s32[2048,1]{0,1:T(1,128)S(1)}, s32[2048,1]{0,1:T(1,128)}, u32[]{:S(2)}) copy-start(s32[2048,1]{0,1:T(1,128)} %copy-done.11) | copy-start | bytes 24580
  321.3 93.5 %all-to-all-start.1 = ((bf16[8,2,160,1536]{3,2,1,0:T(8,128)(2,1)}), bf16[8,2,160,1536]{3,2,1,0:T(8,128)(2,1)}, u32[]{:S(2)}, u32[]{:S(2)}) async-start(bf16[8,2,160,1536]{3,2,1,0:T(8,128)(2,1)} %copy.71), calls=%async_computation.1 | async-start | bytes 15728640 | tf_op jit(solution)/shard_map/all_to_all | solution.py:121
  414.8 34.8 %copy-start.1 = (bf16[2,512,1536]{2,1,0:T(8,128)(2,1)S(1)}, bf16[2,512,1536]{2,1,0:T(8,128)(2,1)}, u32[]{:S(2)}) copy-start(bf16[2,512,1536]{2,1,0:T(8,128)(2,1)} %param.29) | copy-start | bytes 9437188
  432.5 16.0 %copy-start.3 = (f32[256,1536]{1,0:T(8,128)S(1)}, f32[256,1536]{1,0:T(8,128)}, u32[]{:S(2)}) copy-start(f32[256,1536]{1,0:T(8,128)} %copy-done.2) | copy-start | bytes 4718596
Sparse Core Ops, SparseCore 0:
  9.2 35.0 all-gather.5
  46.2 32.3 all-gather.7
  80.2 89.4 all-gather.3
where the time goes:
time: 457 us; the launch traced here: 456 us
  waiting for transfers between devices  198 us (43%)
  blocking collectives  92.1 us (20%)
  local copies, waits for them, and re-layouts  77.5 us (17%)
  matrix products  38.9 us (9%)
  other arithmetic  31 us (7%)
  between operations  13.4 us (3%)
  starting transfers between devices  5.11 us (1%)
    all_to_all x1, blocking collectives, per_device(): lax.all_to_all(outgoing, 'expert', split_axis=0, concat_axis=0, tiled=True)  92.1 us
    all_to_all x1, waiting for transfers between devices, per_device(): lax.all_to_all(run_experts(arrived, expert_gate_weight, expert_up_weight,...  87.9 us
    all_gather x1, waiting for transfers between devices, per_device(): lax.all_gather(attention_output_weight, 'dp', axis=0, tiled=True)  84.1 us
    all_gather x1, waiting for transfers between devices, per_device(): lax.all_gather(adapter_up_factor, 'expert', axis=0, tiled=True)  24 us
    gather x1, local copies, waits for them, and re-layouts, per_device(): jnp.take(came_back.reshape(experts_all * capacity, width), slot_index, ax...  17.7 us
    gather x1, local copies, waits for them, and re-layouts, per_device(): jnp.take(normed, sources, axis=0)  17.6 us
    reduce_sum x1, other arithmetic, per_device(): mixture = jnp.sum(gate_weights[:, :, None] * picked, axis=1)  16 us
    dot_general x1, matrix products, run_experts(): jnp.einsum('secf,efd->secd', active, expert_down_weight, preferred_elemen...  14.2 us
  transfers between devices with their start and end apart: 4, of which 3 were waited for; matrix products, arithmetic and copies ran while one was open for 12% of the time, Pallas kernels for 0%

commit v1 on v0

--- a/solution.py
+++ b/solution.py
@@ -7,6 +7,29 @@
 KV_HEADS = 8
 HEAD = 64
 TOPK = 8
+
+
+def in_blocks(array, dim, peers):
+    shape = array.shape
+    blocks = array.reshape(*shape[:dim], peers, shape[dim] // peers, *shape[dim + 1 :])
+    return jnp.moveaxis(blocks, dim, 0)
+
+
+def laid_out(blocks, dim):
+    blocks = jnp.moveaxis(blocks, 0, dim)
+    dims = blocks.shape
+    return blocks.reshape(*dims[:dim], dims[dim] * dims[dim + 1], *dims[dim + 2 :])
+
+
+def pairwise_exchange(shard, axis, split_dim, concat_dim):
+    size, index = (lax.axis_size(axis), lax.axis_index(axis))
+    blocks = in_blocks(shard, split_dim, size)
+    done = [blocks[index]]
+    for step in range(1, size):
+        sent = blocks[index ^ step]
+        done.append(lax.ppermute(sent, axis, [(i, i ^ step) for i in range(size)]))
+    blocks = jnp.stack(done)[index ^ jnp.arange(size)]
+    return laid_out(blocks, concat_dim)
 
 
 def segment_of(lengths_row, tokens):
@@ -117,7 +140,7 @@
         filled[:, None] > 0, jnp.take(normed, sources, axis=0), jnp.zeros((), normed.dtype)
     )
     outgoing = outgoing.reshape(expert_devices, local_experts, capacity, width)
-    arrived = lax.all_to_all(outgoing, "expert", split_axis=0, concat_axis=0, tiled=True)
+    arrived = pairwise_exchange(outgoing, "expert", 0, 0)
     came_back = lax.all_to_all(
         run_experts(arrived, expert_gate_weight, expert_up_weight, expert_down_weight),
         "expert",

time: 457 us -> 467 us (1.022)
  blocking collectives: 92.1 us -> 0 us
  waiting for transfers between devices: 198 us -> 270 us
  local copies, waits for them, and re-layouts: 77.5 us -> 91.1 us
  starting transfers between devices: 5.11 us -> 12.7 us
  other arithmetic: 31 us -> 36 us
  matrix products: 38.9 us -> 43.7 us
    all_to_all x1 -> x0, blocking collectives: 92.1 us -> none  [per_device(): lax.all_to_all(outgoing, 'expert', split_axis=0, concat_axis=0, tiled=True)]
    ppermute x0 -> x7, waiting for transfers between devices: none -> 77 us  [pairwise_exchange(): done.append(lax.ppermute(sent, axis, [(i, i ^ step) for i in range(size)]))]
    gather x0 -> x1, local copies, waits for them, and re-layouts: none -> 7.72 us  [pairwise_exchange(): blocks = jnp.stack(done)[index ^ jnp.arange(size)]]
    ppermute x0 -> x7, starting transfers between devices: none -> 7.34 us  [pairwise_exchange(): done.append(lax.ppermute(sent, axis, [(i, i ^ step) for i in range(size)]))]
    all_gather x1, waiting for transfers between devices: 24 us -> 18.7 us  [per_device(): lax.all_gather(adapter_up_factor, 'expert', axis=0, tiled=True)]
    dot_general x1, matrix products: 5.91 us -> 10.7 us  [run_experts(): jnp.einsum('secd,edf->secf', arrived, expert_gate_weight, preferred_eleme...]
    unnamed x38 -> x32, local copies, waits for them, and re-layouts: 11.1 us -> 14.1 us
  transfers between devices with their start and end apart: 4 -> 11, of which waited for: 3 -> 6; matrix products, arithmetic and copies ran while one was open for 12% -> 14% of each run, Pallas kernels for 0% -> 0%
where the time goes in v1:
time: 467 us; the launch traced here: 466 us
  waiting for transfers between devices  270 us (58%)
  local copies, waits for them, and re-layouts  91.1 us (20%)
  matrix products  43.7 us (9%)
  other arithmetic  36 us (8%)
  between operations  13.4 us (3%)
  starting transfers between devices  12.7 us (3%)
    all_to_all x1, waiting for transfers between devices, per_device(): lax.all_to_all(run_experts(arrived, expert_gate_weight, expert_up_weight,...  87.8 us
    all_gather x1, waiting for transfers between devices, per_device(): lax.all_gather(attention_output_weight, 'dp', axis=0, tiled=True)  84.1 us
    ppermute x7, waiting for transfers between devices, pairwise_exchange(): done.append(lax.ppermute(sent, axis, [(i, i ^ step) for i in range(size)]))  77 us
    all_gather x1, waiting for transfers between devices, per_device(): lax.all_gather(adapter_up_factor, 'expert', axis=0, tiled=True)  18.7 us
    gather x1, local copies, waits for them, and re-layouts, per_device(): jnp.take(normed, sources, axis=0)  17.9 us
    gather x1, local copies, waits for them, and re-layouts, per_device(): jnp.take(came_back.reshape(experts_all * capacity, width), slot_index, ax...  17.5 us
    reduce_sum x1, other arithmetic, per_device(): mixture = jnp.sum(gate_weights[:, :, None] * picked, axis=1)  16 us
    dot_general x1, matrix products, run_experts(): jnp.einsum('secf,efd->secd', active, expert_down_weight, preferred_elemen...  14.1 us
  transfers between devices with their start and end apart: 11, of which 6 were waited for; matrix products, arithmetic and copies ran while one was open for 14% of the time, Pallas kernels for 0%

profile of v1, /device:TPU:0, one launch (start us, length us, event | category | flops | bytes accessed | tf_op | source)
XLA Modules:
  0.0 466.5 jit_solution(15705039294598872378)
XLA Ops:
  6.5 0.7 all-gather.6.cloned.1.call-update
  7.3 0.7 all-gather.8.cloned.1.call-update
  8.1 0.7 all-gather.4.cloned.1.call-update
  8.7 0.8 copy.62
  9.8 1.3 reduce-window.18
  11.2 2.3 copy.57
  13.5 1.8 copy.56
  15.2 1.8 copy.58
  17.1 4.5 reduce-window.19
  21.6 0.4 slice_reduce_fusion
  22.0 0.2 reduce-window.20
  22.2 0.7 broadcast_multiply_fusion
  23.1 0.7 mul.82
  23.8 0.6 add_select_fusion
  24.5 0.7 compare_select_fusion
  25.3 8.2 %scatter_custom_fusion.1 = s32[2560]{0:T(1024)S(1)} fusion(s32[2048]{0:T(1024)S(1)} %bitcast.151, s32[2048]{0:T(1024)} %add_select_fusion, s32[]{:T(128)} %constant.58.clone.1), kind=kCustom, calls=%fused_computation.90 | custom fusion | bytes 10752 | tf_op jit(solution)/shard_map/scatter | solution.py:137
  33.6 8.1 %scatter_custom_fusion = s32[2560]{0:T(1024)S(1)} fusion(s32[2048]{0:T(1024)S(1)} %bitcast.152, s32[2048]{0:T(1024)S(1)} %broadcast.195, s32[]{:T(128)} %constant.58.clone.1), kind=kCustom, calls=%fused_computation.93 | custom fusion | bytes 10244 | tf_op jit(solution)/shard_map/scatter | solution.py:138
  41.7 0.7 broadcast_in_dim.101
  42.4 0.7 compare_select_fusion.4
  43.0 0.6 pad_clamp_fusion.2
  43.6 0.6 pad_clamp_fusion
  44.2 0.7 convert_reduce_fusion
  44.9 1.1 compare_and_fusion.2
  46.1 0.6 convert_convert_fusion
  46.8 5.9 %fusion.52 = (f32[8,3,256]{2,1,0:T(4,128)S(1)}, f32[8,3,256,256]{2,3,1,0:T(8,128)}) fusion(pred[256,256]{0,1:T(8,128)(4,1)S(1)} %fusion.29, bf16[256,8,64,1]{0,2,3,1:T(8,128)(2,1)} %bitcast.148, bf16[256,8,3,64]{0,3,2,1:T(8,128)(2,1)} %bitcast.145), kind=kOutput, calls=%fused_computation.112 | convolution fusion | flops 207618304 | bytes 7430144 | tf_op jit(solution)/shard_map/sub | solution.py:54
  52.7 4.6 fusion.26
  57.3 2.6 gather_fusion
  59.9 18.7 %all-gather.8.cloned.1.call-done = bf16[64,16,1536]{2,1,0:T(8,128)(2,1)} async-done(((bf16[8,16,1536]{2,1,0:T(8,128)(2,1)}), bf16[64,16,1536]{2,1,0:T(8,128)(2,1)}) %all-gather.8.cloned.1.call-update) | async-done | bytes 3145744 | tf_op jit(solution)/shard_map/all_gather | solution.py:107
  78.5 2.6 gather_fusion.1
  81.1 0.7 broadcast_select_fusion
  81.8 1.4 fusion.53
  83.2 2.3 convolution_bitcast_fusion
  85.5 84.1 %all-gather.4.cloned.1.call-done = bf16[1536,1536]{1,0:T(8,128)(2,1)} async-done(((bf16[384,1536]{1,0:T(8,128)(2,1)}), bf16[1536,1536]{1,0:T(8,128)(2,1)}) %all-gather.4.cloned.1.call-update) | async-done | bytes 4718608 | tf_op jit(solution)/shard_map/all_gather | solution.py:99
  169.6 4.8 %multiply_reduce_fusion.1 = (f32[256]{0:T(256)S(1)}, f32[256,1536]{1,0:T(8,128)S(1)}) fusion(f32[256,1536]{1,0:T(8,128)} %convolution_bitcast_fusion, bf16[256,1536]{0,1:T(8,128)(2,1)} %bitcast.143, bf16[1536,1536]{1,0:T(8,128)(2,1)} %all-gather.4.cloned.1.call-done, bf16[256,1536]{1,0:T(8,128)(2,1)} %param.18), kind=kOutput, calls=%fused_computation.39 | convolution fusion | flops 1209925376 | bytes 9438208 | tf_op jit(solution)/shard_map/dot_general | solution.py:97
  174.4 1.1 copy-done.1
  175.5 1.1 multiply_convert_fusion
  176.6 17.9 %gather_fusion.2 = bf16[2560,1536]{1,0:T(8,128)(2,1)} fusion(bf16[256,1536]{1,0:T(8,128)(2,1)} %multiply_convert_fusion, s32[3072]{0:T(1024)S(1)} %copy-done.6), kind=kCustom, calls=%fused_computation.2 | custom fusion | bytes 15738880 | tf_op jit(solution)/shard_map/jit(_take)/gather | solution.py:140
  194.5 4.5 select_select_fusion
  198.9 1.7 dynamic-slice_bitcast_fusion
  200.6 1.5 collective-permute-start.1
  202.1 0.4 collective-permute-start.2
  202.5 1.5 collective-permute-start.3
  204.2 2.4 collective-permute-start.5
  206.6 1.0 bitcast_dynamic-update-slice_fusion.6
  207.6 17.5 %collective-permute-done.1 = bf16[1,2,160,1536]{3,2,1,0:T(8,128)(2,1)S(1)} collective-permute-done((bf16[1,2,160,1536]{3,2,1,0:T(8,128)(2,1)S(1)}, bf16[1,2,160,1536]{3,2,1,0:T(8,128)(2,1)S(1)}, u32[]{:S(2)}, u32[]{:S(2)}) %collective-permute-start.1) | collective-permute-done | bytes 983072 | tf_op jit(solution)/shard_map/ppermute | solution.py:30
  225.1 1.4 collective-permute-start.6
  226.5 1.0 bitcast_dynamic-update-slice_fusion.5
  227.5 17.9 %collective-permute-done.2 = bf16[1,2,160,1536]{3,2,1,0:T(8,128)(2,1)S(1)} collective-permute-done((bf16[1,2,160,1536]{3,2,1,0:T(8,128)(2,1)S(1)}, bf16[1,2,160,1536]{3,2,1,0:T(8,128)(2,1)S(1)}, u32[]{:S(2)}, u32[]{:S(2)}) %collective-permute-start.2) | collective-permute-done | bytes 983072 | tf_op jit(solution)/shard_map/ppermute | solution.py:30
  245.4 1.0 bitcast_dynamic-update-slice_fusion.4
  246.5 1.0 bitcast_dynamic-update-slice_fusion.3
  247.5 41.5 %collective-permute-done.4 = bf16[1,2,160,1536]{3,2,1,0:T(8,128)(2,1)S(1)} collective-permute-done((bf16[1,2,160,1536]{3,2,1,0:T(8,128)(2,1)S(1)}, bf16[1,2,160,1536]{3,2,1,0:T(8,128)(2,1)S(1)}, u32[]{:S(2)}, u32[]{:S(2)}) %collective-permute-start.4) | collective-permute-done | bytes 983072 | tf_op jit(solution)/shard_map/ppermute | solution.py:30
  289.0 1.0 bitcast_dynamic-update-slice_fusion.2
  290.1 1.0 bitcast_dynamic-update-slice_fusion.1
  291.1 1.1 bitcast_dynamic-update-slice_fusion
  292.2 7.7 %gather_fusion.3 = bf16[8,2,160,1536]{3,2,1,0:T(8,128)(2,1)} fusion(bf16[8,2,160,1536]{3,2,1,0:T(8,128)(2,1)} %bitcast.35, s32[1024]{0:T(1024)S(1)} %pad_clamp_fusion.1), kind=kCustom, calls=%fused_computation.3 | custom fusion | bytes 15728672 | tf_op jit(solution)/shard_map/gather | solution.py:31
  299.9 10.7 %fusion.3 = f32[2,8,160,512]{3,2,1,0:T(8,128)} fusion(bf16[8,2,160,1536]{3,2,1,0:T(8,128)(2,1)} %gather_fusion.3, bf16[2,1536,512]{2,1,0:T(8,128)(2,1)} %param.27), kind=kOutput, calls=%fused_computation.13 | convolution fusion | flops 4026531840 | bytes 16252928 | tf_op jit(solution)/shard_map/secd,edf->secf/dot_general | solution.py:63
  310.6 14.1 %convert_bitcast_fusion = bf16[8,2,160,1536]{3,2,0,1:T(8,128)(2,1)} fusion(bf16[2,512,1536]{2,1,0:T(8,128)(2,1)S(1)} %copy-done, f32[2,8,160,512]{3,2,1,0:T(8,128)} %fusion.3, bf16[2,1536,512]{2,1,0:T(8,128)(2,1)} %param.28, bf16[8,2,160,1536]{3,2,1,0:T(8,128)(2,1)} %gather_fusion.3), kind=kOutput, calls=%fused_computation.9 | convolution fusion | flops 8064860160 | bytes 27262976 | tf_op jit(solution)/shard_map/secf,efd->secd/dot_general | solution.py:70
  324.7 7.0 %copy.69 = bf16[8,2,160,1536]{3,2,1,0:T(8,128)(2,1)} copy(bf16[8,2,160,1536]{3,2,0,1:T(8,128)(2,1)} %convert_bitcast_fusion) | data formatting | bytes 15728640 | tf_op jit(solution)/shard_map/convert_element_type | solution.py:72
  331.7 5.2 %all-to-all-start = ((bf16[8,2,160,1536]{3,2,1,0:T(8,128)(2,1)}), bf16[8,2,160,1536]{3,2,1,0:T(8,128)(2,1)}, u32[]{:S(2)}, u32[]{:S(2)}) async-start(bf16[8,2,160,1536]{3,2,1,0:T(8,128)(2,1)} %copy.69), calls=%async_computation | async-start | bytes 15728640 | tf_op jit(solution)/shard_map/all_to_all | solution.py:144
  337.1 0.2 copy.65
  337.5 87.8 %all-to-all-done = bf16[8,2,160,1536]{3,2,1,0:T(8,128)(2,1)} async-done(((bf16[8,2,160,1536]{3,2,1,0:T(8,128)(2,1)}), bf16[8,2,160,1536]{3,2,1,0:T(8,128)(2,1)}, u32[]{:S(2)}, u32[]{:S(2)}) %all-to-all-start) | async-done | bytes 7864352 | tf_op jit(solution)/shard_map/all_to_all | solution.py:144
  425.3 17.5 %gather_fusion.4 = bf16[2048,1536]{1,0:T(8,128)(2,1)} fusion(bf16[2560,1536]{1,0:T(8,128)(2,1)} %bitcast.46, s32[2048]{0:T(1024)S(1)} %broadcast_clamp_fusion), kind=kCustom, calls=%fused_computation.4 | custom fusion | bytes 12591104 | tf_op jit(solution)/shard_map/jit(_take)/gather | solution.py:151
  442.9 16.0 %multiply_reduce_fusion = f32[256,1536]{1,0:T(8,128)S(1)} fusion(bf16[2048,1536]{1,0:T(8,128)(2,1)} %gather_fusion.4, f32[256,8]{1,0:T(8,128)S(1)} %copy.61, pred[256,8]{1,0:T(8,128)(4,1)S(1)} %copy.65), kind=kLoop, calls=%fused_computation.8 | loop fusion | flops 12189696 | bytes 7874560 | tf_op jit(solution)/shard_map/reduce_sum | solution.py:154
  458.9 1.1 add_convert_fusion
  (54 shorter events, 1.3 us)
Async XLA Ops:
  6.5 304.1 %copy-start = (bf16[2,512,1536]{2,1,0:T(8,128)(2,1)S(1)}, bf16[2,512,1536]{2,1,0:T(8,128)(2,1)}, u32[]{:S(2)}) copy-start(bf16[2,512,1536]{2,1,0:T(8,128)(2,1)} %param.29) | copy-start | bytes 9437188
  6.5 50.7 %all-gather.6.cloned.1.call-start = ((), (), s32[]{:S(2)}) async-start(), calls=%async_computation.2 | async-start | bytes 3538944 | tf_op jit(solution)/shard_map/all_gather | solution.py:106
  7.3 71.3 %all-gather.8.cloned.1.call-start = ((), (), s32[]{:S(2)}) async-start(), calls=%async_computation.3 | async-start | bytes 3538944 | tf_op jit(solution)/shard_map/all_gather | solution.py:107
  8.0 161.6 %all-gather.4.cloned.1.call-start = ((), (), s32[]{:S(2)}) async-start(), calls=%async_computation.1 | async-start | bytes 5898240 | tf_op jit(solution)/shard_map/all_gather | solution.py:99
  23.8 28.9 %copy-start.3 = (bf16[256,512]{0,1:T(8,128)(2,1)S(1)}, bf16[256,512]{0,1:T(8,128)(2,1)}, u32[]{:S(2)}) copy-start(bf16[256,512]{0,1:T(8,128)(2,1)} %copy.58) | copy-start | bytes 786436
  25.3 20.8 %copy-start.8 = (s32[2048,1]{0,1:T(1,128)}, s32[2048,1]{0,1:T(1,128)S(1)}, u32[]{:S(2)}) copy-start(s32[2048,1]{0,1:T(1,128)S(1)} %compare_select_fusion) | copy-start | bytes 24580
  85.5 90.1 %copy-start.10 = (f32[1536]{0:T(1024)S(1)}, f32[1536]{0:T(1024)}, u32[]{:S(2)}) copy-start(f32[1536]{0:T(1024)} %param.24) | copy-start | bytes 18436
  85.5 91.1 %copy-start.6 = (s32[3072]{0:T(1024)S(1)}, s32[3072]{0:T(1024)}, u32[]{:S(2)}) copy-start(s32[3072]{0:T(1024)} %pad_clamp_fusion) | copy-start | bytes 36868
  174.3 1.2 copy-start.1
  176.6 17.9 %copy-start.7 = (pred[8,2,160]{2,1,0:T(4,128)(4,1)S(1)}, pred[8,2,160]{2,1,0:T(4,128)(4,1)}, u32[]{:S(2)}) copy-start(pred[8,2,160]{2,1,0:T(4,128)(4,1)} %broadcast_in_dim.101) | copy-start | bytes 7684
  200.6 3.6 collective-permute-start
  200.6 24.6 %collective-permute-start.1 = (bf16[1,2,160,1536]{3,2,1,0:T(8,128)(2,1)S(1)}, bf16[1,2,160,1536]{3,2,1,0:T(8,128)(2,1)S(1)}, u32[]{:S(2)}, u32[]{:S(2)}) collective-permute-start(bf16[1,2,160,1536]{3,2,1,0:T(8,128)(2,1)S(1)} %get-tuple-element.10), channel_id=1, source_target_pairs={{0,2},{1,3},{2,0},{3,1},{4,6},{5,7},{6,4},{7,5},{8,10},{9,11},{10,... | collective-permute-start | bytes 2949128 | tf_op jit(solution)/shard_map/ppermute | solution.py:30
  202.1 43.3 %collective-permute-start.2 = (bf16[1,2,160,1536]{3,2,1,0:T(8,128)(2,1)S(1)}, bf16[1,2,160,1536]{3,2,1,0:T(8,128)(2,1)S(1)}, u32[]{:S(2)}, u32[]{:S(2)}) collective-permute-start(bf16[1,2,160,1536]{3,2,1,0:T(8,128)(2,1)S(1)} %get-tuple-element.9), channel_id=1, source_target_pairs={{0,3},{1,2},{2,1},{3,0},{4,7},{5,6},{6,5},{7,4},{8,11},{9,10},{10,... | collective-permute-start | bytes 2949128 | tf_op jit(solution)/shard_map/ppermute | solution.py:30
  202.5 43.9 %collective-permute-start.3 = (bf16[1,2,160,1536]{3,2,1,0:T(8,128)(2,1)S(1)}, bf16[1,2,160,1536]{3,2,1,0:T(8,128)(2,1)S(1)}, u32[]{:S(2)}, u32[]{:S(2)}) collective-permute-start(bf16[1,2,160,1536]{3,2,1,0:T(8,128)(2,1)S(1)} %get-tuple-element.8), channel_id=1, source_target_pairs={{0,4},{1,5},{2,6},{3,7},{4,0},{5,1},{6,2},{7,3},{8,12},{9,13},{10,... | collective-permute-start | bytes 2949128 | tf_op jit(solution)/shard_map/ppermute | solution.py:30
  204.0 85.0 %collective-permute-start.4 = (bf16[1,2,160,1536]{3,2,1,0:T(8,128)(2,1)S(1)}, bf16[1,2,160,1536]{3,2,1,0:T(8,128)(2,1)S(1)}, u32[]{:S(2)}, u32[]{:S(2)}) collective-permute-start(bf16[1,2,160,1536]{3,2,1,0:T(8,128)(2,1)S(1)} %get-tuple-element.7), channel_id=1, source_target_pairs={{0,5},{1,4},{2,7},{3,6},{4,1},{5,0},{6,3},{7,2},{8,13},{9,12},{10,... | collective-permute-start | bytes 2949128 | tf_op jit(solution)/shard_map/ppermute | solution.py:30
  204.2 85.9 %collective-permute-start.5 = (bf16[1,2,160,1536]{3,2,1,0:T(8,128)(2,1)S(1)}, bf16[1,2,160,1536]{3,2,1,0:T(8,128)(2,1)S(1)}, u32[]{:S(2)}, u32[]{:S(2)}) collective-permute-start(bf16[1,2,160,1536]{3,2,1,0:T(8,128)(2,1)S(1)} %get-tuple-element.6), channel_id=1, source_target_pairs={{0,6},{1,7},{2,4},{3,5},{4,2},{5,3},{6,0},{7,1},{8,14},{9,15},{10,... | collective-permute-start | bytes 2949128 | tf_op jit(solution)/shard_map/ppermute | solution.py:30
  225.1 66.0 %collective-permute-start.6 = (bf16[1,2,160,1536]{3,2,1,0:T(8,128)(2,1)S(1)}, bf16[1,2,160,1536]{3,2,1,0:T(8,128)(2,1)S(1)}, u32[]{:S(2)}, u32[]{:S(2)}) collective-permute-start(bf16[1,2,160,1536]{3,2,1,0:T(8,128)(2,1)S(1)} %get-tuple-element.5), channel_id=1, source_target_pairs={{0,7},{1,6},{2,5},{3,4},{4,3},{5,2},{6,1},{7,0},{8,15},{9,14},{10,... | collective-permute-start | bytes 2949128 | tf_op jit(solution)/shard_map/ppermute | solution.py:30
  331.7 5.4 %copy-start.4 = (s32[256,8]{0,1:T(8,128)S(1)}, s32[256,8]{0,1:T(8,128)}, u32[]{:S(2)}) copy-start(s32[256,8]{0,1:T(8,128)} %param.26) | copy-start | bytes 24580
  331.7 5.6 %copy-start.5 = (f32[256,8]{0,1:T(8,128)S(1)}, f32[256,8]{0,1:T(8,128)}, u32[]{:S(2)}) copy-start(f32[256,8]{0,1:T(8,128)} %param.25) | copy-start | bytes 24580
  331.7 5.8 %copy-start.9 = (s32[2048,1]{0,1:T(1,128)S(1)}, s32[2048,1]{0,1:T(1,128)}, u32[]{:S(2)}) copy-start(s32[2048,1]{0,1:T(1,128)} %copy-done.8) | copy-start | bytes 24580
  331.7 93.6 %all-to-all-start = ((bf16[8,2,160,1536]{3,2,1,0:T(8,128)(2,1)}), bf16[8,2,160,1536]{3,2,1,0:T(8,128)(2,1)}, u32[]{:S(2)}, u32[]{:S(2)}) async-start(bf16[8,2,160,1536]{3,2,1,0:T(8,128)(2,1)} %copy.69), calls=%async_computation | async-start | bytes 15728640 | tf_op jit(solution)/shard_map/all_to_all | solution.py:144
  442.9 16.0 %copy-start.2 = (f32[256,1536]{1,0:T(8,128)S(1)}, f32[256,1536]{1,0:T(8,128)}, u32[]{:S(2)}) copy-start(f32[256,1536]{1,0:T(8,128)} %copy-done.1) | copy-start | bytes 4718596
Sparse Core Ops, SparseCore 0:
  9.2 35.0 all-gather.5
  46.2 32.3 all-gather.7
  80.1 89.4 all-gather.3
